TPU v7x, 256 devices: a whole 4x4x8 slice. The times are simulated.
256 devices in a mesh: prompt: 16 (over z, core), comp: 16 (over x, y).
Axes of the slice: x: 4, y: 4, z: 8, core: 2. Of those that a mesh axis runs over, the one named last changes fastest.
Arguments:
- prompt_inner: bfloat16 [4096, 16384], P('prompt', 'comp'), may hold values from -0.59765625 to 0.59765625
- prompt_proj: bfloat16 [4096, 4096], P('prompt'), may hold values from -0.8984375 to 0.8984375
- prompt_step: float32 [256, 4096], P('comp', 'prompt')
- completion_inner: bfloat16 [32, 256, 16384], P('comp', None, 'prompt'), may hold values from -0.59765625 to 0.59765625
- completion_gate: bfloat16 [32, 256, 16384], P('comp', None, 'prompt'), may hold values from -12 to 12
- completion_projections: bfloat16 [32, 256, 4096], P('comp'), may hold values from -0.8984375 to 0.8984375
- sample_step: float32 [256, 32, 256], P('prompt', 'comp')
- sample_length: int32 [32], P('comp'), may hold values from 1 to 256, as said below
- decay_log: float32 [256], replicated
- conv_inner: bfloat16 [4, 16384], replicated, may hold values from -3 to 3
- conv_proj: bfloat16 [4, 4096], replicated, may hold values from -3 to 3
- norm_gain: float32 [16384], P('prompt'), may hold values from 0.5 to 1.5
Outputs:
- sample_out: bfloat16 [32, 256, 16384], P('comp', None, 'prompt')
Inputs may be any that keep to these rules, and one draw needn't show every extreme that they name: `sample_length`: some completion slot is full.
All inputs are finite; a program needn't handle non-finite values.
Results may differ from a plain program's by a relative error of at most 0.014.
Values may be sent and summed in bfloat16 or wider, within the bound.
A program may use at most 128 MiB of HBM per device.

v0:
```python
import jax
import jax.numpy as jnp
from jax import lax
from jax.sharding import PartitionSpec as P

STATE_HEADS = 256
HEAD_WIDTH = 64
STATE_WIDTH = 256
STATE_GROUPS = 8
CONV = 4
BLOCK = 128
EPS = 1e-05
HIGHEST = lax.Precision.HIGHEST


def from_behind(block, axis, distance):
    devices = range(lax.axis_size(axis))
    route = [(i - distance, i) for i in devices if i - distance in devices]
    return lax.ppermute(block, axis, route)


def carried_in(array, axis, combine, identity):
    peers, position = (lax.axis_size(axis), lax.axis_index(axis))
    everything = jax.tree.map(
        lambda part, kind: lax.all_gather(part.astype(kind), axis),
        array,
        (jnp.bfloat16, jnp.bfloat16),
    )
    start = jax.tree.map(
        lambda part, zero: jnp.broadcast_to(jnp.asarray(zero, part.dtype), part.shape),
        array,
        identity,
    )

    def hop(k, before):
        reached = k < position
        new = combine(
            before, jax.tree.map(lambda part, own: part[k].astype(own.dtype), everything, array)
        )
        return jax.tree.map(lambda a, b: jnp.where(reached, a, b), new, before)

    return lax.fori_loop(0, peers, hop, start)


def from_root(array, axis, root):
    mine = lax.axis_index(axis) == root
    return lax.psum(jnp.where(mine, array, jnp.zeros_like(array)), axis)


def from_partner(block, axis, stride):
    count = lax.axis_size(axis)
    route = []
    for low in range(count):
        high = low | 1 << stride
        if high != low and high < count:
            route += [(low, high), (high, low)]
    return lax.ppermute(block, axis, route)


def causal_conv(source, kernel, leading):
    padded = jnp.concatenate([leading, source], axis=0).astype(jnp.float32)
    kernel_wide = kernel.astype(jnp.float32)
    row_count = source.shape[0]
    summed = jnp.zeros(source.shape, jnp.float32)
    for offset in range(kernel.shape[0]):
        summed = summed + kernel_wide[offset] * padded[offset : offset + row_count]
    return jax.nn.silu(summed).astype(jnp.bfloat16)


def block_scan(state_in, inner_blk, b_blk, c_blk, step_blk, rate_vals):
    cumul = jnp.cumsum(-rate_vals[:, :, None] * step_blk, axis=2)
    scores = jnp.einsum("ign,jgn->gij", c_blk, b_blk, preferred_element_type=jnp.float32)
    spread_log = cumul[:, :, :, None] - cumul[:, :, None, :]
    length_q = step_blk.shape[2]
    causal = jnp.arange(length_q)[:, None] >= jnp.arange(length_q)[None, :]
    decay_mat = jnp.exp(jnp.where(causal, spread_log, -jnp.inf))
    mixer_w = (scores[:, None] * decay_mat * step_blk[:, :, None, :]).astype(jnp.bfloat16)
    intra_part = jnp.einsum(
        "gkij,jgkd->igkd", mixer_w, inner_blk, preferred_element_type=jnp.float32
    )
    readout = jnp.einsum("ign,gkdn->igkd", c_blk.astype(jnp.float32), state_in, precision=HIGHEST)
    inter_part = jnp.transpose(jnp.exp(cumul), (2, 0, 1))[..., None] * readout
    weights = jnp.exp(cumul[:, :, -1:] - cumul) * step_blk
    packed = (inner_blk.astype(jnp.float32) * jnp.transpose(weights, (2, 0, 1))[..., None]).astype(
        jnp.bfloat16
    )
    fresh_part = jnp.einsum("jgn,jgkd->gkdn", b_blk, packed, preferred_element_type=jnp.float32)
    return (
        intra_part + inter_part,
        jnp.exp(cumul[:, :, -1])[..., None, None] * state_in + fresh_part,
    )


def local(
    prompt_inner,
    prompt_proj,
    prompt_step,
    completion_inner,
    completion_gate,
    completion_projections,
    sample_step,
    sample_length,
    decay_log,
    conv_inner,
    conv_proj,
    norm_gain,
):
    prompt_count = lax.axis_size("prompt")
    prompt_idx = lax.axis_index("prompt")
    column_idx = lax.axis_index("comp")
    heads_group = STATE_HEADS // STATE_GROUPS
    heads_col = prompt_step.shape[0]
    heads_row = sample_step.shape[0]
    state_feats = STATE_GROUPS * STATE_WIDTH
    lag_rows = CONV - 1
    rows_prompt = prompt_inner.shape[0]
    prev_inner, prev_proj = from_behind(
        (
            prompt_inner[rows_prompt - lag_rows :],
            prompt_proj[rows_prompt - lag_rows :, :state_feats],
        ),
        "prompt",
        1,
    )
    col_start = column_idx * heads_col
    conv_col = lax.dynamic_slice_in_dim(
        conv_inner, col_start * HEAD_WIDTH, heads_col * HEAD_WIDTH, 1
    )
    inner_conv = causal_conv(prompt_inner, conv_col, prev_inner)
    b_conv = causal_conv(prompt_proj[:, :state_feats], conv_proj[:, :state_feats], prev_proj)
    rate_col = jnp.exp(lax.dynamic_slice_in_dim(decay_log, col_start, heads_col, 0))
    step_col = jax.nn.softplus(prompt_step)
    cumul = jnp.cumsum(-rate_col[:, None] * step_col, axis=1)
    local_log = cumul[:, -1]
    weight_col = jnp.exp(local_log[:, None] - cumul) * step_col
    group_span = max(1, heads_col // heads_group)
    per_group = heads_col // group_span
    group_start = col_start // heads_group
    b_select = lax.dynamic_slice_in_dim(
        b_conv.reshape(rows_prompt, STATE_GROUPS, STATE_WIDTH), group_start, group_span, 1
    ).astype(jnp.float32)
    scaled = (
        inner_conv.astype(jnp.float32).reshape(rows_prompt, heads_col, HEAD_WIDTH)
        * jnp.transpose(weight_col)[:, :, None]
    )
    scaled = scaled.reshape(rows_prompt, group_span, per_group, HEAD_WIDTH)
    local_state = jnp.einsum("tgn,tghd->ghdn", b_select, scaled, precision=HIGHEST).reshape(
        heads_col, HEAD_WIDTH, STATE_WIDTH
    )
    own_inner = prompt_inner[rows_prompt - lag_rows :].astype(jnp.float32)
    own_proj = prompt_proj[rows_prompt - lag_rows :].astype(jnp.float32)
    last_index = prompt_count - 1
    head_start = prompt_idx * heads_row
    owner = head_start // heads_col

    def combine(earlier, later):
        return (earlier[0] + later[0], earlier[1] * jnp.exp(later[0])[:, None, None] + later[1])

    before = carried_in(
        (local_log, local_state),
        "prompt",
        combine,
        (jnp.zeros_like(local_log), jnp.zeros_like(local_state)),
    )
    through = combine(before, (local_log, local_state))[1]
    final_state, tail_inner, tail_proj = (
        from_root(through.astype(jnp.bfloat16), "prompt", last_index).astype(through.dtype),
        from_root(own_inner.astype(jnp.bfloat16), "prompt", last_index).astype(own_inner.dtype),
        from_root(own_proj.astype(jnp.bfloat16), "prompt", last_index).astype(own_proj.dtype),
    )
    moved_state, moved_inner = (
        from_root(final_state.astype(jnp.bfloat16), "comp", owner).astype(final_state.dtype),
        from_root(tail_inner.astype(jnp.bfloat16), "comp", owner).astype(tail_inner.dtype),
    )
    lead_inner = moved_inner.astype(jnp.bfloat16)
    group_row = head_start // heads_group
    b_start = group_row * STATE_WIDTH
    c_start = state_feats + group_row * STATE_WIDTH
    proj_select = jnp.concatenate(
        [
            lax.dynamic_slice_in_dim(completion_projections, b_start, STATE_WIDTH, 2),
            lax.dynamic_slice_in_dim(completion_projections, c_start, STATE_WIDTH, 2),
        ],
        axis=2,
    )
    kernel_select = jnp.concatenate(
        [
            lax.dynamic_slice_in_dim(conv_proj, b_start, STATE_WIDTH, 1),
            lax.dynamic_slice_in_dim(conv_proj, c_start, STATE_WIDTH, 1),
        ],
        axis=1,
    )
    lead_wide = tail_proj.astype(jnp.bfloat16)
    lead_select = jnp.concatenate(
        [
            lax.dynamic_slice_in_dim(lead_wide, b_start, STATE_WIDTH, 1),
            lax.dynamic_slice_in_dim(lead_wide, c_start, STATE_WIDTH, 1),
        ],
        axis=1,
    )
    conv_row = lax.dynamic_slice_in_dim(
        conv_inner, head_start * HEAD_WIDTH, heads_row * HEAD_WIDTH, 1
    )
    rate_row = jnp.exp(lax.dynamic_slice_in_dim(decay_log, head_start, heads_row, 0))
    step_row = jax.nn.softplus(sample_step)
    slot_count = completion_inner.shape[0]
    sample_len = completion_inner.shape[1]
    block_count = sample_len // BLOCK

    def advance(carry, block_in):
        block_out, carry_next = block_scan(
            carry, block_in[0], block_in[1], block_in[2], block_in[3], rate_row[None]
        )
        return (carry_next, block_out)

    gated_list = []
    square_list = []
    for slot in range(slot_count):
        slot_conv = causal_conv(completion_inner[slot], conv_row, lead_inner)
        proj_conv = causal_conv(proj_select[slot], kernel_select, lead_select)
        inner_blocks = slot_conv.reshape(block_count, BLOCK, 1, heads_row, HEAD_WIDTH)
        b_blocks = proj_conv[:, :STATE_WIDTH].reshape(block_count, BLOCK, 1, STATE_WIDTH)
        c_blocks = proj_conv[:, STATE_WIDTH:].reshape(block_count, BLOCK, 1, STATE_WIDTH)
        step_blocks = jnp.transpose(
            step_row[:, slot].reshape(heads_row, block_count, BLOCK), (1, 0, 2)
        )[:, None]
        block_inputs = (inner_blocks, b_blocks, c_blocks, step_blocks)
        _, block_outs = lax.scan(advance, moved_state[None], block_inputs)
        ssm_out = block_outs.reshape(sample_len, heads_row * HEAD_WIDTH)
        gated = ssm_out * jax.nn.silu(completion_gate[slot].astype(jnp.float32))
        gated_list.append(gated)
        square_list.append(jnp.sum(gated * gated, axis=1))
    square_all = jnp.stack(square_list)
    square_all = square_all + from_partner(square_all, "prompt", 0)
    scale_all = lax.rsqrt(square_all / (heads_group * HEAD_WIDTH) + EPS)
    gated_all = jnp.stack(gated_list)
    result = gated_all * scale_all[:, :, None] * norm_gain[None, None, :]
    live_rows = jnp.arange(sample_len)[None, :] < sample_length[:, None]
    return jnp.where(live_rows[:, :, None], result, 0.0).astype(jnp.bfloat16)


def solution(mesh):
    placed = (
        P("prompt", "comp"),
        P("prompt", None),
        P("comp", "prompt"),
        P("comp", None, "prompt"),
        P("comp", None, "prompt"),
        P("comp", None, None),
        P("prompt", "comp", None),
        P("comp"),
        P(),
        P(),
        P(),
        P("prompt"),
    )
    return jax.shard_map(
        local, mesh=mesh, in_specs=placed, out_specs=P("comp", None, "prompt"), check_vma=False
    )
```

profile of v0, /device:TPU:1, one launch (start us, length us, event | category | flops | bytes accessed | tf_op | source)
XLA Modules:
  0.0 410.7 jit_solution(14466374462376283287)
XLA Ops:
  7.3 4.9 %collective-permute-start = (bf16[3,1024]{1,0:T(4,128)(2,1)S(1)}, bf16[3,1024]{1,0:T(4,128)(2,1)S(1)}, u32[]{:S(2)}, u32[]{:S(2)}) collective-permute-start(bf16[3,1024]{1,0:T(4,128)(2,1)S(1)} %get-tuple-element.414), channel_id=1, source_target_pairs={{0,16},{16,32},{32,48},{48,64},{64,80},{80,96},{96,112},{112,128},... | collective-permute-start | bytes 18440 | tf_op jit(solution)/shard_map/ppermute | solution.py:19
  13.0 1.9 collective-permute-start.1
  22.2 1.6 bitcast_multiply_fusion
  30.2 46.1 %all-reduce.1 = (bf16[256]{0:T(256)(128)(2,1)S(1)}, bf16[3,1024]{1,0:T(4,128)(2,1)S(1)}, bf16[3,4096]{1,0:T(4,128)(2,1)S(1)}) all-reduce(bf16[256]{0:T(256)(128)(2,1)S(1)} %dynamic-update-slice, bf16[3,1024]{1,0:T(4,128)(2,1)S(1)} %get-tuple-element.413, ...), channel_id=2, replica_groups=mesh['prompt'=16,'comp'=16] {'prompt'}, use_global_device_ids=true, to_apply=%add | all-reduce | flops 15616 | bytes 62464
  76.4 35.3 %psum.38 = bf16[3,1024]{1,0:T(4,128)(2,1)S(1)} all-reduce(bf16[3,1024]{1,0:T(4,128)(2,1)S(1)} %broadcast_select_fusion.1), channel_id=1, replica_groups=mesh['prompt'=16,'comp'=16] {'comp'}, use_global_device_ids=true, to_apply=%region_7.8 | all-reduce | flops 3072 | bytes 12288 | tf_op jit(solution)/shard_map/psum | solution.py:47
  111.9 2.1 fusion.99
  119.7 2.4 multiply_convert_fusion.8
  122.1 21.4 %while.44 = (s32[]{:T(128)}, f32[16,64,256]{2,1,0:T(8,128)S(1)}, s32[]{:T(128)}, bf16[16,16]{1,0:T(8,128)(2,1)S(1)}, bf16[16,16,64,256]{3,2,1,0:T(8,128)(2,1)}, /*index=5*/s32[]{:T(128)}, s32[]{:T(128)}) while((s32[]{:T(128)}, f32[16,64,256]{2,1,0:T(8,128)S(1)}, s32[]{:T(128)}, bf16[16,16]{1,0:T(8,128)(2,1)S(1)}, ...), condition=%wide.region_3.4_spmd.clone, body=%wide.region_2.3_spmd.clone.sunk | while | flops 1310740 | bytes 2621713 | solution.py:42
  144.9 2.1 fusion.98
  146.9 114.7 %all-reduce.5.cloned.1.call-done = bf16[16,64,256]{2,1,0:T(8,128)(2,1)} async-done(((bf16[16,64,256]{2,1,0:T(8,128)(2,1)}), bf16[16,64,256]{2,1,0:T(8,128)(2,1)}) %all-reduce.5.cloned.1.call-update) | async-done | bytes 524304 | tf_op jit(solution)/shard_map/psum | solution.py:47
  267.0 2.1 convert_element_type.228
  269.0 2.1 convert_element_type.223
  272.4 87.0 %all-reduce.7.cloned.1.call-done = bf16[1,16,64,256]{3,2,1,0:T(8,128)(2,1)} async-done(((bf16[1,16,64,256]{3,2,1,0:T(8,128)(2,1)}), bf16[1,16,64,256]{3,2,1,0:T(8,128)(2,1)}) %all-reduce.7.cloned.1.call-update) | async-done | bytes 524304 | tf_op jit(solution)/shard_map/psum | solution.py:47
  361.8 16.0 %while.43 = (s32[]{:T(128)}, f32[1,16,64,256]{3,2,1,0:T(8,128)S(1)}, f32[2,128,1,16,64]{1,4,3,2,0:T(8,128)}, f32[1,16,1]{1,2,0:T(1,128)}, f32[2,1,16,128]{3,0,2,...) while((s32[]{:T(128)}, ...), condition=%wide.region_14.15_spmd, body=%wide.region_12.14_spmd.sunk | while | flops 514478080 | bytes 16805992 | solution.py:228
  365.0 1.6 fusion.151
  366.6 1.4 fusion.150
  373.0 1.6 fusion.151
  377.8 2.1 copy.80
  379.9 3.0 fusion.72
  383.1 8.1 %while.42 = (s32[]{:T(128)}, f32[1,16,64,256]{3,2,1,0:T(8,128)S(1)}, f32[2,128,1,16,64]{1,4,3,2,0:T(8,128)S(1)}, f32[1,16,1]{1,2,0:T(1,128)}, f32[2,1,16,128]{3,...) while((s32[]{:T(128)}, ...), condition=%wide.region_11.12_spmd, body=%wide.region_9.11_spmd.sunk | while | flops 514478080 | bytes 7893013 | solution.py:228
  393.5 2.3 collective-permute-start.2
  395.8 2.2 fusion.71
  398.1 3.6 fusion.70
  401.7 2.5 copy.86
  (198 shorter events, 73.1 us)
Async XLA Ops:
  6.5 115.6 %all-gather.4.cloned.1.call-start = ((), (), s32[]{:S(2)}) async-start(), calls=%async_computation.2 | async-start | bytes 8912896 | tf_op jit(solution)/shard_map/all_gather | solution.py:25
  7.3 14.4 %collective-permute-start = (bf16[3,1024]{1,0:T(4,128)(2,1)S(1)}, bf16[3,1024]{1,0:T(4,128)(2,1)S(1)}, u32[]{:S(2)}, u32[]{:S(2)}) collective-permute-start(bf16[3,1024]{1,0:T(4,128)(2,1)S(1)} %get-tuple-element.414), channel_id=1, source_target_pairs={{0,16},{16,32},{32,48},{48,64},{64,80},{80,96},{96,112},{112,128},... | collective-permute-start | bytes 18440 | tf_op jit(solution)/shard_map/ppermute | solution.py:19
  13.0 10.9 %collective-permute-start.1 = (bf16[3,2048]{1,0:T(4,128)(2,1)S(1)}, bf16[3,2048]{1,0:T(4,128)(2,1)S(1)}, u32[]{:S(2)}, u32[]{:S(2)}) collective-permute-start(bf16[3,2048]{1,0:T(4,128)(2,1)S(1)} %slice.215), channel_id=1, source_target_pairs={{0,16},{16,32},{32,48},{48,64},{64,80},{80,96},{96,112},{112,128},... | collective-permute-start | bytes 36872 | tf_op jit(solution)/shard_map/ppermute | solution.py:19
  27.5 234.1 %all-reduce.5.cloned.1.call-start = ((), (), s32[]{:S(2)}) async-start(), calls=%async_computation | async-start | bytes 1048576 | tf_op jit(solution)/shard_map/psum | solution.py:47
  144.6 117.8 %copy-start.17 = (s32[2]{0:T(128)S(1)}, s32[2]{0:T(128)}, u32[]{:S(2)}) copy-start(s32[2]{0:T(128)} %param.25) | copy-start | bytes 28
  144.6 214.8 %all-reduce.7.cloned.1.call-start = ((), (), s32[]{:S(2)}) async-start(), calls=%async_computation.1 | async-start | bytes 1048576 | tf_op jit(solution)/shard_map/psum | solution.py:47
  264.1 2.0 copy-start.11
  264.9 4.1 copy-start
  267.0 4.8 %copy-start.12 = (bf16[256,512]{1,0:T(8,128)(2,1)S(1)}, bf16[256,512]{1,0:T(8,128)(2,1)}, u32[]{:S(2)}) copy-start(bf16[256,512]{1,0:T(8,128)(2,1)} %get-tuple-element.444) | copy-start | bytes 786436
  364.7 3.3 copy-start.7
  365.0 3.2 copy-start.2
  365.0 3.3 copy-start.6
  372.7 3.3 copy-start.7
  373.0 3.2 copy-start.2
  373.0 3.2 copy-start.6
  377.8 2.1 copy-start.1
  379.9 3.2 copy-start.13
  384.3 2.3 copy-start.5
  388.4 2.3 copy-start.5
  391.2 1.9 copy-start.9
  393.5 4.6 %copy-start.8 = (f32[1,256,1024]{1,0,2:T(1,128)S(1)}, f32[1,256,1024]{1,0,2:T(1,128)}, u32[]{:S(2)}) copy-start(f32[1,256,1024]{1,0,2:T(1,128)} %fusion.72) | copy-start | bytes 3145732
  393.5 4.6 %copy-start.15 = (f32[1024]{0:T(1024)S(1)}, f32[1024]{0:T(1024)}, u32[]{:S(2)}) copy-start(f32[1024]{0:T(1024)} %param.29) | copy-start | bytes 12292
  393.5 4.6 %copy-start.16 = (pred[2,256]{1,0:T(4,128)(4,1)S(1)}, pred[2,256]{1,0:T(4,128)(4,1)}, u32[]{:S(2)}) copy-start(pred[2,256]{1,0:T(4,128)(4,1)} %iota_compare_fusion.2) | copy-start | bytes 1540
  393.5 4.5 %collective-permute-start.2 = (f32[2,256]{1,0:T(2,128)S(1)}, f32[2,256]{1,0:T(2,128)S(1)}, u32[]{:S(2)}, u32[]{:S(2)}) collective-permute-start(f32[2,256]{1,0:T(2,128)S(1)} %pad_maximum_fusion.4), channel_id=1, source_target_pairs={{0,16},{16,0},{32,48},{48,32},{64,80},{80,64},{96,112},{112,96},{1... | collective-permute-start | bytes 6152 | tf_op jit(solution)/shard_map/ppermute | solution.py:57
  (7 other events, 8.9 us)
Sparse Core Ops, SparseCore 0:
  27.6 58.7 all-gather.3
  144.7 116.7 all-reduce.4
  265.1 94.3 all-reduce.6
where the time goes:
time: 413 us; the launch traced here: 411 us
  waiting for transfers between devices  202 us (49%)
  blocking collectives  81.4 us (20%)
  other arithmetic  59.8 us (14%)
  local copies, waits for them, and re-layouts  29 us (7%)
  between operations  14.3 us (3%)
  matrix products  14.2 us (3%)
  starting transfers between devices  9.41 us (2%)
    psum x2, waiting for transfers between devices, from_root(): return lax.psum(jnp.where(mine, array, jnp.zeros_like(array)), axis)  202 us
    unnamed x1, blocking collectives  46.1 us
    psum x1, blocking collectives, from_root(): return lax.psum(jnp.where(mine, array, jnp.zeros_like(array)), axis)  35.3 us
    select_n x16, other arithmetic, hop(): return jax.tree.map(lambda a, b: jnp.where(reached, a, b), new, before)  20.7 us
  transfers between devices with their start and end apart: 6, of which 2 were waited for; matrix products, arithmetic and copies ran while one was open for 9% of the time, Pallas kernels for 0%

commit v1 on v0

--- a/solution.py
+++ b/solution.py
@@ -44,7 +44,7 @@
 
 def from_root(array, axis, root):
     mine = lax.axis_index(axis) == root
-    return lax.psum(jnp.where(mine, array, jnp.zeros_like(array)), axis)
+    return jnp.sum(jax.lax.all_gather(jnp.where(mine, array, jnp.zeros_like(array)), axis), axis=0)
 
 
 def from_partner(block, axis, stride):

time: 413 us -> 302 us (0.73)
  waiting for transfers between devices: 202 us -> 85.9 us
  other arithmetic: 59.8 us -> 68.8 us
    psum x2 -> x0, waiting for transfers between devices: 202 us -> none  [from_root(): return lax.psum(jnp.where(mine, array, jnp.zeros_like(array)), axis)]
    all_gather x0 -> x3, blocking collectives: none -> 55.8 us  [from_root(): jax.lax.all_gather(jnp.where(mine, array, jnp.zeros_like(array)), axis)]
    all_gather x0 -> x2, waiting for transfers between devices: none -> 54.5 us  [from_root(): jax.lax.all_gather(jnp.where(mine, array, jnp.zeros_like(array)), axis)]
    psum x1 -> x0, blocking collectives: 35.3 us -> none  [from_root(): return lax.psum(jnp.where(mine, array, jnp.zeros_like(array)), axis)]
    all_gather x1, waiting for transfers between devices: 0.02 us -> 31.3 us  [carried_in(): lax.all_gather(part.astype(kind), axis)]
    unnamed x1, blocking collectives: 46.1 us -> 25.3 us
    reduce_sum x0 -> x5, other arithmetic: none -> 10.9 us  [from_root(): jnp.sum(jax.lax.all_gather(jnp.where(mine, array, jnp.zeros_like(array)),...]
  transfers between devices with their start and end apart: 6 -> 6, of which waited for: 2 -> 2; matrix products, arithmetic and copies ran while one was open for 9% -> 11% of each run, Pallas kernels for 0% -> 0%
where the time goes in v1:
time: 302 us; the launch traced here: 300 us
  waiting for transfers between devices  85.9 us (28%)
  blocking collectives  81.1 us (27%)
  other arithmetic  68.8 us (23%)
  local copies, waits for them, and re-layouts  27.1 us (9%)
  between operations  14.3 us (5%)
  matrix products  14.2 us (5%)
  starting transfers between devices  7.16 us (2%)
    all_gather x3, blocking collectives, from_root(): jax.lax.all_gather(jnp.where(mine, array, jnp.zeros_like(array)), axis)  55.8 us
    all_gather x2, waiting for transfers between devices, from_root(): jax.lax.all_gather(jnp.where(mine, array, jnp.zeros_like(array)), axis)  54.5 us
    all_gather x1, waiting for transfers between devices, carried_in(): lax.all_gather(part.astype(kind), axis)  31.3 us
    unnamed x1, blocking collectives  25.3 us
    select_n x16, other arithmetic, hop(): return jax.tree.map(lambda a, b: jnp.where(reached, a, b), new, before)  20.7 us
    reduce_sum x5, other arithmetic, from_root(): jnp.sum(jax.lax.all_gather(jnp.where(mine, array, jnp.zeros_like(array)),...  10.9 us
    ppermute x2, starting transfers between devices, from_behind(): return lax.ppermute(block, axis, route)  6.86 us
  transfers between devices with their start and end apart: 6, of which 2 were waited for; matrix products, arithmetic and copies ran while one was open for 11% of the time, Pallas kernels for 0%

profile of v1, /device:TPU:1, one launch (start us, length us, event | category | flops | bytes accessed | tf_op | source)
XLA Modules:
  0.0 299.6 jit_solution(12301456681415351991)
XLA Ops:
  7.3 4.9 %collective-permute-start = (bf16[3,1024]{1,0:T(4,128)(2,1)S(1)}, bf16[3,1024]{1,0:T(4,128)(2,1)S(1)}, u32[]{:S(2)}, u32[]{:S(2)}) collective-permute-start(bf16[3,1024]{1,0:T(4,128)(2,1)S(1)} %get-tuple-element.427), channel_id=1, source_target_pairs={{0,16},{16,32},{32,48},{48,64},{64,80},{80,96},{96,112},{112,128},... | collective-permute-start | bytes 18440 | tf_op jit(solution)/shard_map/ppermute | solution.py:19
  13.0 1.9 collective-permute-start.1
  22.4 1.6 bitcast_multiply_fusion
  29.4 25.3 %all-reduce = bf16[256]{0:T(256)(128)(2,1)S(1)} all-reduce(bf16[256]{0:T(256)(128)(2,1)S(1)} %dynamic-update-slice), channel_id=2, replica_groups=mesh['prompt'=16,'comp'=16] {'prompt'}, use_global_device_ids=true, to_apply=%add | all-reduce | flops 256 | bytes 1024
  54.8 31.3 %all-gather.14.cloned.1.call-done = bf16[256,64,256]{2,1,0:T(8,128)(2,1)} async-done(((bf16[16,64,256]{2,1,0:T(8,128)(2,1)}), bf16[256,64,256]{2,1,0:T(8,128)(2,1)}) %all-gather.14.cloned.1.call-update) | async-done | bytes 8388624 | tf_op jit(solution)/shard_map/all_gather | solution.py:25
  86.1 21.4 %while.44 = (s32[]{:T(128)}, f32[16,64,256]{2,1,0:T(8,128)S(1)}, s32[]{:T(128)}, bf16[16,16]{1,0:T(8,128)(2,1)S(1)}, bf16[16,16,64,256]{3,2,1,0:T(8,128)(2,1)}, /*index=5*/s32[]{:T(128)}, s32[]{:T(128)}) while((s32[]{:T(128)}, f32[16,64,256]{2,1,0:T(8,128)S(1)}, s32[]{:T(128)}, bf16[16,16]{1,0:T(8,128)(2,1)S(1)}, ...), condition=%wide.region_3.4_spmd.clone, body=%wide.region_2.3_spmd.clone.sunk | while | flops 1310740 | bytes 2621713 | solution.py:42
  108.7 54.5 %all-gather.16.cloned.1.call-done = bf16[256,64,256]{2,1,0:T(8,128)(2,1)} async-done(((bf16[16,64,256]{2,1,0:T(8,128)(2,1)}), bf16[256,64,256]{2,1,0:T(8,128)(2,1)}) %all-gather.16.cloned.1.call-update) | async-done | bytes 8388624 | tf_op jit(solution)/shard_map/all_gather | solution.py:47
  163.2 5.3 %reduce_sum.78 = bf16[16,64,256]{2,1,0:T(8,128)(2,1)S(1)} reduce(bf16[16,16,64,256]{3,2,1,0:T(8,128)(2,1)} %bitcast.290, bf16[]{:T(256)} %constant.169.clone.1), dimensions={0}, to_apply=%region_4.5 | reduce | flops 3932160 | bytes 8912898 | tf_op jit(solution)/shard_map/reduce_sum | solution.py:47
  169.3 15.9 %all-gather.7 = bf16[16,3,1024]{2,1,0:T(4,128)(2,1)S(1)} all-gather(bf16[1,3,1024]{2,1,0:T(4,128)(2,1)S(1)} %get-tuple-element.426), channel_id=6, replica_groups=mesh['prompt'=16,'comp'=16] {'prompt'}, dimensions={0}, use_global_device_ids=true | all-gather | bytes 104448 | tf_op jit(solution)/shard_map/all_gather | solution.py:47
  185.3 19.0 %all-gather.8 = bf16[16,3,1024]{2,1,0:T(4,128)(2,1)S(1)} all-gather(bf16[1,3,1024]{2,1,0:T(4,128)(2,1)S(1)} %select_bitcast_fusion.1), channel_id=7, replica_groups=mesh['prompt'=16,'comp'=16] {'comp'}, dimensions={0}, use_global_device_ids=true | all-gather | bytes 104448 | tf_op jit(solution)/shard_map/all_gather | solution.py:47
  205.8 2.4 multiply_convert_fusion.8
  209.2 2.0 copy.95
  211.2 20.8 %all-gather.9 = bf16[16,3,4096]{2,1,0:T(4,128)(2,1)S(1)} all-gather(bf16[1,3,4096]{2,1,0:T(4,128)(2,1)S(1)} %select_bitcast_fusion), channel_id=8, replica_groups=mesh['prompt'=16,'comp'=16] {'prompt'}, dimensions={0}, use_global_device_ids=true | all-gather | bytes 417792 | tf_op jit(solution)/shard_map/all_gather | solution.py:47
  236.6 2.1 convert_element_type.252
  238.7 2.0 convert_element_type.247
  245.5 5.3 %reduce_sum.79 = bf16[16,64,256]{2,1,0:T(8,128)(2,1)S(1)} reduce(bf16[16,16,64,256]{3,2,1,0:T(8,128)(2,1)} %bitcast.289, bf16[]{:T(256)} %constant.169.clone.1), dimensions={0}, to_apply=%region_5.6 | reduce | flops 3932160 | bytes 8912898 | tf_op jit(solution)/shard_map/reduce_sum | solution.py:47
  252.1 16.2 %while.43 = (s32[]{:T(128)}, f32[1,16,64,256]{3,2,1,0:T(8,128)S(1)}, f32[2,128,1,16,64]{1,4,3,2,0:T(8,128)}, f32[1,16,1]{1,2,0:T(1,128)}, f32[2,1,16,128]{3,0,2,...) while((s32[]{:T(128)}, ...), condition=%wide.region_14.15_spmd, body=%wide.region_12.14_spmd.sunk | while | flops 514478080 | bytes 16805992 | solution.py:228
  255.4 1.6 fusion.151
  268.3 2.1 copy.96
  270.5 3.0 %fusion.72 = f32[1,256,1024]{1,0,2:T(1,128)} fusion(f32[1,256,1024]{1,0,2:T(1,128)S(1)} %bitcast.298, bf16[1,256,1024]{1,0,2:T(2,128)(2,1)S(1)} %copy-done.1), kind=kLoop, calls=%fused_computation.103 | loop fusion | flops 1572864 | bytes 2621440 | tf_op jit(solution)/shard_map/mul | solution.py:230
  273.6 8.6 %while.42 = (s32[]{:T(128)}, f32[1,16,64,256]{3,2,1,0:T(8,128)S(1)}, f32[2,128,1,16,64]{1,4,3,2,0:T(8,128)S(1)}, f32[1,16,1]{1,2,0:T(1,128)}, f32[2,1,16,128]{3,...) while((s32[]{:T(128)}, ...), condition=%wide.region_11.12_spmd, body=%wide.region_9.11_spmd.sunk | while | flops 514478080 | bytes 7893013 | solution.py:228
  284.7 2.2 fusion.71
  287.0 3.6 %fusion.70 = bf16[2,256,1024]{1,0,2:T(2,128)(2,1)S(1)} fusion(f32[1,256,1024]{1,0,2:T(1,128)S(1)} %copy-done.8, f32[1,256,1024]{1,0,2:T(1,128)S(1)} %fusion.71, pred[2,256]{1,0:T(4,128)(4,1)S(1)} %copy-done.16, f32[1024]{0:T(1024)S(1)} %copy-done.15, f32[2,256]{1,0:T(2,128)S(1)} %add_rsqrt_fusion), kind=kLoop, calls=%fused_computation.98 | loop fusion | flops 2621440 | bytes 3152384 | tf_op jit(solution)/shard_map/convert_element_type | solution.py:239
  290.6 2.5 copy.102
  (205 shorter events, 74.8 us)
Async XLA Ops:
  6.5 79.6 %all-gather.14.cloned.1.call-start = ((), (), s32[]{:S(2)}) async-start(), calls=%async_computation | async-start | bytes 8912896 | tf_op jit(solution)/shard_map/all_gather | solution.py:25
  7.3 14.5 %collective-permute-start = (bf16[3,1024]{1,0:T(4,128)(2,1)S(1)}, bf16[3,1024]{1,0:T(4,128)(2,1)S(1)}, u32[]{:S(2)}, u32[]{:S(2)}) collective-permute-start(bf16[3,1024]{1,0:T(4,128)(2,1)S(1)} %get-tuple-element.427), channel_id=1, source_target_pairs={{0,16},{16,32},{32,48},{48,64},{64,80},{80,96},{96,112},{112,128},... | collective-permute-start | bytes 18440 | tf_op jit(solution)/shard_map/ppermute | solution.py:19
  13.0 11.0 %collective-permute-start.1 = (bf16[3,2048]{1,0:T(4,128)(2,1)S(1)}, bf16[3,2048]{1,0:T(4,128)(2,1)S(1)}, u32[]{:S(2)}, u32[]{:S(2)}) collective-permute-start(bf16[3,2048]{1,0:T(4,128)(2,1)S(1)} %slice.215), channel_id=1, source_target_pairs={{0,16},{16,32},{32,48},{48,64},{64,80},{80,96},{96,112},{112,128},... | collective-permute-start | bytes 36872 | tf_op jit(solution)/shard_map/ppermute | solution.py:19
  27.6 135.6 %all-gather.16.cloned.1.call-start = ((), (), s32[]{:S(2)}) async-start(), calls=%async_computation.1 | async-start | bytes 8912896 | tf_op jit(solution)/shard_map/all_gather | solution.py:47
  108.6 136.9 %all-gather.18.cloned.1.call-start = ((), (), s32[]{:S(2)}) async-start(), calls=%async_computation.2 | async-start | bytes 8912896 | tf_op jit(solution)/shard_map/all_gather | solution.py:47
  168.5 36.2 %copy-start.12 = (bf16[2,256,1024]{2,1,0:T(8,128)(2,1)S(1)}, bf16[2,256,1024]{2,1,0:T(8,128)(2,1)}, u32[]{:S(2)}) copy-start(bf16[2,256,1024]{2,1,0:T(8,128)(2,1)} %param.21) | copy-start | bytes 3145732
  208.2 2.9 copy-start.9
  234.6 4.1 %copy-start = (bf16[1,256,1024]{1,0,2:T(2,128)(2,1)}, bf16[1,256,1024]{1,0,2:T(2,128)(2,1)S(1)}, u32[]{:S(2)}) copy-start(bf16[1,256,1024]{1,0,2:T(2,128)(2,1)S(1)} %copy.109) | copy-start | bytes 1572868
  240.7 2.0 copy-start.17
  240.8 2.7 copy-start.14
  255.2 3.3 %copy-start.7 = (bf16[2,128,1,256]{3,1,2,0:T(8,128)(2,1)S(1)}, bf16[2,128,1,256]{3,1,2,0:T(8,128)(2,1)}, u32[]{:S(2)}) copy-start(bf16[2,128,1,256]{3,1,2,0:T(8,128)(2,1)} %get-tuple-element.659) | copy-start | bytes 393220 | tf_op jit(solution)/shard_map/while
  255.4 3.2 %copy-start.2 = (f32[2,128,1,16,64]{1,4,3,2,0:T(8,128)S(1)}, f32[2,128,1,16,64]{1,4,3,2,0:T(8,128)}, u32[]{:S(2)}) copy-start(f32[2,128,1,16,64]{1,4,3,2,0:T(8,128)} %get-tuple-element.644) | copy-start | bytes 3145732 | tf_op jit(solution)/shard_map/while
  255.4 3.3 %copy-start.6 = (bf16[2,128,1,16,64]{1,4,3,2,0:T(8,128)(2,1)S(1)}, bf16[2,128,1,16,64]{1,4,3,2,0:T(8,128)(2,1)}, u32[]{:S(2)}) copy-start(bf16[2,128,1,16,64]{1,4,3,2,0:T(8,128)(2,1)} %get-tuple-element.657) | copy-start | bytes 1572868 | tf_op jit(solution)/shard_map/while
  263.3 3.3 %copy-start.7 = (bf16[2,128,1,256]{3,1,2,0:T(8,128)(2,1)S(1)}, bf16[2,128,1,256]{3,1,2,0:T(8,128)(2,1)}, u32[]{:S(2)}) copy-start(bf16[2,128,1,256]{3,1,2,0:T(8,128)(2,1)} %get-tuple-element.659) | copy-start | bytes 393220 | tf_op jit(solution)/shard_map/while
  263.5 3.2 %copy-start.2 = (f32[2,128,1,16,64]{1,4,3,2,0:T(8,128)S(1)}, f32[2,128,1,16,64]{1,4,3,2,0:T(8,128)}, u32[]{:S(2)}) copy-start(f32[2,128,1,16,64]{1,4,3,2,0:T(8,128)} %get-tuple-element.644) | copy-start | bytes 3145732 | tf_op jit(solution)/shard_map/while
  263.5 3.2 %copy-start.6 = (bf16[2,128,1,16,64]{1,4,3,2,0:T(8,128)(2,1)S(1)}, bf16[2,128,1,16,64]{1,4,3,2,0:T(8,128)(2,1)}, u32[]{:S(2)}) copy-start(bf16[2,128,1,16,64]{1,4,3,2,0:T(8,128)(2,1)} %get-tuple-element.657) | copy-start | bytes 1572868 | tf_op jit(solution)/shard_map/while
  268.3 2.1 copy-start.1
  270.5 3.1 %copy-start.13 = (f32[16,1,256]{2,1,0:T(1,128)S(1)}, f32[16,1,256]{2,1,0:T(1,128)}, u32[]{:S(2)}) copy-start(f32[16,1,256]{2,1,0:T(1,128)} %get-tuple-element.436) | copy-start | bytes 49156
  275.0 2.3 copy-start.5
  279.1 2.3 copy-start.5
  284.5 2.5 copy-start.8
  284.5 2.5 copy-start.15
  284.5 2.5 copy-start.16
  284.5 2.4 collective-permute-start.2
  (7 other events, 10.0 us)
Sparse Core Ops, SparseCore 0:
  27.7 58.3 all-gather.13
  108.7 54.4 all-gather.15
  169.4 74.0 all-gather.17
